TPU v7x, 32 devices: a whole 2x2x4 slice. The times are simulated.
32 devices in a mesh: gx: 8 (over z, core), gy: 4 (over y, x).
Axes of the slice: x: 2, y: 2, z: 4, core: 2. Of those that a mesh axis runs over, the one named last changes fastest.
Arguments:
- rhs_field: float32 [128, 64, 128], P('gx', 'gy'), may hold values from -10 to 10
- diag_blocks: bfloat16 [128, 64, 128, 128], P('gx', 'gy'), may hold values from -1 to 4, as said below
- face_lift: bfloat16 [4, 128, 128], replicated, may hold values from -0.5 to 0.5
- face_state: int32 [128, 64, 4], P('gx', 'gy'), may hold values from 0 to 2
- restrict_basis: float32 [128, 8], replicated, may hold values from -0.5 to 0.5
- coarse_inverse: float32 [128, 64, 8, 8], P('gx', 'gy'), may hold values from -0.4 to 1.2
Outputs:
- solution_field: float32 [128, 64, 128], P('gx', 'gy')
- hessenberg: float32 [3, 2], replicated
Inputs may be any that keep to these rules, and one draw needn't show every extreme that they name: `diag_blocks`: each block has diagonal entries between 2 and 4 and small off-diagonal entries.
All inputs are finite; a program needn't handle non-finite values.
Results may differ from a plain program's by a relative error of at most 0.0023.
Values may be sent and summed in bfloat16 or wider, within the bound.
A program may use at most 64 MiB of HBM per device.

v0:
```python
import jax
import jax.numpy as jnp
from jax import lax
from jax.sharding import PartitionSpec as P


def padded_2(block, sides, width):
    for axis, dim in sides:
        count = lax.axis_size(axis)
        forward = [(i, i + 1) for i in range(count - 1)]
        backward = [(target, source) for source, target in forward]
        low = lax.ppermute(
            lax.slice_in_dim(block, block.shape[dim] - width, None, axis=dim), axis, forward
        )
        high = lax.ppermute(lax.slice_in_dim(block, 0, width, axis=dim), axis, backward)
        block = jnp.concatenate([low, block, high], axis=dim)
    return block


def apply_operator(field, diag_blocks, face_lift, face_state):
    rounded = field.astype(jnp.bfloat16)
    local_part = jnp.einsum(
        "ija,ijab->ijb", rounded, diag_blocks, preferred_element_type=jnp.float32
    )
    padded = padded_2(rounded, (("gx", 0), ("gy", 1)), 1)
    neighbours = [padded[:-2, 1:-1], padded[2:, 1:-1], padded[1:-1, :-2], padded[1:-1, 2:]]
    zero_block = jnp.zeros_like(rounded)
    selected = []
    for face in range(4):
        state = face_state[:, :, face][:, :, None]
        other = neighbours[face]
        selected.append(
            jnp.where(state == 1, other, jnp.where(state == 2, other[:, :, ::-1], zero_block))
        )
    stacked = jnp.concatenate(selected, axis=-1)
    width = rounded.shape[2]
    lifted = jnp.dot(
        stacked.reshape(-1, 4 * width),
        face_lift.reshape(4 * width, width),
        preferred_element_type=jnp.float32,
    )
    return local_part + lifted.reshape(field.shape)


def coarse_correct(field, restrict_basis, coarse_inverse):
    high = lax.Precision.HIGHEST
    coarse = jnp.einsum("ija,ak->ijk", field, restrict_basis, precision=high)
    rows_y = coarse.shape[1]
    column = lax.all_gather(coarse, "gy", axis=1, tiled=True)
    centred = column - jnp.mean(column, axis=1, keepdims=True)
    padded = jnp.pad(centred, ((0, 0), (1, 1), (0, 0)))
    smoothed_all = centred + 0.25 * (padded[:, :-2] + padded[:, 2:])
    start = lax.axis_index("gy") * rows_y
    smoothed = lax.dynamic_slice_in_dim(smoothed_all, start, rows_y, 1)
    solved = jnp.einsum("ijk,ijkl->ijl", smoothed, coarse_inverse, precision=high)
    return field + jnp.einsum("ijl,al->ija", solved, restrict_basis, precision=high)


def least_squares(start_len, hess):
    first = jnp.sqrt(hess[0, 0] ** 2 + hess[1, 0] ** 2)
    cos_one = hess[0, 0] / first
    sin_one = hess[1, 0] / first
    upper = cos_one * hess[0, 1] + sin_one * hess[1, 1]
    lower = -sin_one * hess[0, 1] + cos_one * hess[1, 1]
    second = jnp.sqrt(lower**2 + hess[2, 1] ** 2)
    cos_two = lower / second
    coef_two = cos_two * (-sin_one * start_len) / second
    coef_one = (cos_one * start_len - upper * coef_two) / first
    return (coef_one, coef_two)


def body(rhs_field, diag_blocks, face_lift, face_state, restrict_basis, coarse_inverse):
    start_len = jnp.sqrt(lax.psum(jnp.sum(rhs_field * rhs_field), ("gx", "gy")))
    basis = [rhs_field / start_len]
    precon = []
    hess = jnp.zeros((3, 2), jnp.float32)
    for step in range(2):
        precond = coarse_correct(basis[step], restrict_basis, coarse_inverse)
        precon.append(precond)
        image = apply_operator(precond, diag_blocks, face_lift, face_state)
        partial_dots = jnp.stack([jnp.sum(vector * image) for vector in basis])
        coeffs = lax.psum(partial_dots, ("gx", "gy"))
        for index in range(step + 1):
            image = image - coeffs[index] * basis[index]
        length = jnp.sqrt(lax.psum(jnp.sum(image * image), ("gx", "gy")))
        for index in range(step + 1):
            hess = hess.at[index, step].set(coeffs[index])
        hess = hess.at[step + 1, step].set(length)
        if step == 0:
            basis.append(image / length)
    coef_one, coef_two = least_squares(start_len, hess)
    return (coef_one * precon[0] + coef_two * precon[1], hess)


def solution(mesh):
    in_specs = (
        P("gx", "gy", None),
        P("gx", "gy", None, None),
        P(),
        P("gx", "gy", None),
        P(),
        P("gx", "gy", None, None),
    )
    out_specs = (P("gx", "gy", None), P())
    return jax.shard_map(body, mesh=mesh, in_specs=in_specs, out_specs=out_specs, check_vma=False)
```

profile of v0, /device:TPU:0, one launch (start us, length us, event | category | flops | bytes accessed | tf_op | source)
XLA Modules:
  0.0 293.5 jit_solution(4230740229205972593)
XLA Ops:
  0.6 1.6 multiply_reduce_fusion.7
  2.2 42.2 %psum.35 = f32[]{:T(128)} all-reduce(f32[]{:T(128)} %multiply_reduce_fusion.7), channel_id=1, replica_groups=mesh['gx'=8,'gy'=4] {'gx','gy'}, use_global_device_ids=true, to_apply=%region_1.0 | all-reduce | flops 1 | bytes 8 | tf_op jit(solution)/shard_map/psum | solution.py:73
  45.1 0.9 broadcast_divide_fusion.1
  46.0 1.7 fusion.20
  47.7 10.3 %all_gather.6 = f32[16,64,8]{0,2,1:T(8,128)S(1)} all-gather(f32[16,16,8]{0,2,1:T(8,128)S(1)} %fusion.20), channel_id=1, replica_groups=mesh['gx'=8,'gy'=4] {'gy'}, dimensions={1}, use_global_device_ids=true | all-gather | bytes 40960 | tf_op jit(solution)/shard_map/all_gather | solution.py:49
  58.3 1.1 multiply_reduce_fusion.1
  59.4 1.1 fusion.36
  60.5 1.3 collective-permute-start
  61.8 1.3 collective-permute-start.1
  63.1 0.9 fusion.32
  64.1 5.7 %fusion.18 = f32[16,16,1,128]{3,2,1,0:T(1,128)S(1)} fusion(bf16[16,16,128,128]{3,2,1,0:T(8,128)(2,1)} %param.17, bf16[16,16,128,1]{2,1,0,3:T(8,128)(2,1)S(1)} %bitcast.67), kind=kOutput, calls=%fused_computation.28 | convolution fusion | flops 8388608 | bytes 8585216 | tf_op jit(solution)/shard_map/ija,ijab->ijb/dot_general | solution.py:22
  69.9 2.5 collective-permute-start.2
  72.4 1.3 collective-permute-start.3
  73.7 4.2 %collective-permute-done.3 = bf16[18,1,128]{2,1,0:T(2,128)(2,1)S(1)} collective-permute-done((bf16[18,1,128]{2,1,0:T(2,128)(2,1)S(1)}, bf16[18,1,128]{2,1,0:T(2,128)(2,1)S(1)}, u32[]{:S(2)}, u32[]{:S(2)}) %collective-permute-start.3) | collective-permute-done | bytes 4640 | tf_op jit(solution)/shard_map/ppermute | solution.py:15
  78.9 0.8 multiply_reduce_fusion.6
  79.7 42.8 %psum.36 = f32[1]{0:T(128)} all-reduce(f32[1]{0:T(128)} %bitcast.14), channel_id=1, replica_groups=mesh['gx'=8,'gy'=4] {'gx','gy'}, use_global_device_ids=true, to_apply=%region_4.5 | all-reduce | flops 1 | bytes 8 | tf_op jit(solution)/shard_map/psum | solution.py:82
  122.5 1.3 multiply_reduce_fusion.5
  123.8 40.7 %psum.37 = f32[]{:T(128)} all-reduce(f32[]{:T(128)} %multiply_reduce_fusion.5), channel_id=1, replica_groups=mesh['gx'=8,'gy'=4] {'gx','gy'}, use_global_device_ids=true, to_apply=%region_6.7 | all-reduce | flops 1 | bytes 8 | tf_op jit(solution)/shard_map/psum | solution.py:85
  165.8 1.0 fusion.16
  166.9 10.3 %all_gather.7 = f32[16,64,8]{0,2,1:T(8,128)S(1)} all-gather(f32[16,16,8]{0,2,1:T(8,128)S(1)} %fusion.16), channel_id=1, replica_groups=mesh['gx'=8,'gy'=4] {'gy'}, dimensions={1}, use_global_device_ids=true | all-gather | bytes 40960 | tf_op jit(solution)/shard_map/all_gather | solution.py:49
  177.9 1.3 collective-permute-start.4
  179.2 1.3 collective-permute-start.5
  181.2 2.9 collective-permute-done.5
  184.1 2.0 collective-permute-start.6
  186.2 1.3 collective-permute-start.7
  187.5 5.7 %fusion.14 = f32[16,16,1,128]{3,2,1,0:T(1,128)S(1)} fusion(bf16[16,16,128,128]{3,2,1,0:T(8,128)(2,1)} %param.17, bf16[16,16,128,1]{2,1,0,3:T(8,128)(2,1)S(1)} %bitcast.68), kind=kOutput, calls=%fused_computation.24 | convolution fusion | flops 8388608 | bytes 8585216 | tf_op jit(solution)/shard_map/ija,ijab->ijb/dot_general | solution.py:22
  194.2 0.9 multiply_reduce_fusion.4
  195.1 1.3 pad_maximum_fusion.22
  197.1 42.6 %psum.38 = f32[2]{0:T(128)S(1)} all-reduce(f32[2]{0:T(128)S(1)} %pad_maximum_fusion.22), channel_id=1, replica_groups=mesh['gx'=8,'gy'=4] {'gx','gy'}, use_global_device_ids=true, to_apply=%region_10.11 | all-reduce | flops 2 | bytes 16 | tf_op jit(solution)/shard_map/psum | solution.py:82
  240.3 2.0 multiply_reduce_fusion.2
  242.3 39.8 %psum.39 = f32[]{:T(128)} all-reduce(f32[]{:T(128)} %multiply_reduce_fusion.2), channel_id=1, replica_groups=mesh['gx'=8,'gy'=4] {'gx','gy'}, use_global_device_ids=true, to_apply=%region_12.13 | all-reduce | flops 1 | bytes 8 | tf_op jit(solution)/shard_map/psum | solution.py:85
  282.8 1.9 scatter.20
  (64 shorter events, 8.0 us)
Async XLA Ops:
  0.6 78.2 %copy-start = (bf16[4,128,128]{2,1,0:T(8,128)(2,1)S(1)}, bf16[4,128,128]{2,1,0:T(8,128)(2,1)}, u32[]{:S(2)}) copy-start(bf16[4,128,128]{2,1,0:T(8,128)(2,1)} %param.18) | copy-start | bytes 393220
  60.5 9.3 %collective-permute-start = (bf16[1,16,128]{2,1,0:T(8,128)(2,1)S(1)}, bf16[1,16,128]{2,1,0:T(8,128)(2,1)S(1)}, u32[]{:S(2)}, u32[]{:S(2)}) collective-permute-start(bf16[1,16,128]{2,1,0:T(8,128)(2,1)S(1)} %get-tuple-element.82), channel_id=1, source_target_pairs={{0,4},{4,8},{8,12},{12,16},{16,20},{20,24},{24,28},{1,5},{5,9},{9,... | collective-permute-start | bytes 12296 | tf_op jit(solution)/shard_map/ppermute | solution.py:12
  61.8 8.1 %collective-permute-start.1 = (bf16[1,16,128]{2,1,0:T(8,128)(2,1)S(1)}, bf16[1,16,128]{2,1,0:T(8,128)(2,1)S(1)}, u32[]{:S(2)}, u32[]{:S(2)}) collective-permute-start(bf16[1,16,128]{2,1,0:T(8,128)(2,1)S(1)} %get-tuple-element.83), channel_id=1, source_target_pairs={{4,0},{8,4},{12,8},{16,12},{20,16},{24,20},{28,24},{5,1},{9,5},{13... | collective-permute-start | bytes 12296 | tf_op jit(solution)/shard_map/ppermute | solution.py:15
  64.1 58.4 %copy-start.1 = (f32[16,16,128]{2,1,0:T(8,128)S(1)}, f32[16,16,128]{2,1,0:T(8,128)}, u32[]{:S(2)}) copy-start(f32[16,16,128]{2,1,0:T(8,128)} %param.16) | copy-start | bytes 393220
  64.1 101.7 %copy-start.3 = (f32[128,8]{0,1:T(8,128)S(1)}, f32[128,8]{0,1:T(8,128)}, u32[]{:S(2)}) copy-start(f32[128,8]{0,1:T(8,128)} %param.20) | copy-start | bytes 12292
  64.1 113.3 %copy-start.2 = (f32[16,16,8,8]{1,3,2,0:T(8,128)S(1)}, f32[16,16,8,8]{1,3,2,0:T(8,128)}, u32[]{:S(2)}) copy-start(f32[16,16,8,8]{1,3,2,0:T(8,128)} %param.21) | copy-start | bytes 196612
  69.9 3.8 %collective-permute-start.2 = (bf16[18,1,128]{2,1,0:T(2,128)(2,1)S(1)}, bf16[18,1,128]{2,1,0:T(2,128)(2,1)S(1)}, u32[]{:S(2)}, u32[]{:S(2)}) collective-permute-start(bf16[18,1,128]{2,1,0:T(2,128)(2,1)S(1)} %get-tuple-element.74), channel_id=1, source_target_pairs={{0,1},{1,2},{2,3},{4,5},{5,6},{6,7},{8,9},{9,10},{10,11},{12,13},{... | collective-permute-start | bytes 13832 | tf_op jit(solution)/shard_map/ppermute | solution.py:12
  72.4 5.6 %collective-permute-start.3 = (bf16[18,1,128]{2,1,0:T(2,128)(2,1)S(1)}, bf16[18,1,128]{2,1,0:T(2,128)(2,1)S(1)}, u32[]{:S(2)}, u32[]{:S(2)}) collective-permute-start(bf16[18,1,128]{2,1,0:T(2,128)(2,1)S(1)} %get-tuple-element.75), channel_id=1, source_target_pairs={{1,0},{2,1},{3,2},{5,4},{6,5},{7,6},{9,8},{10,9},{11,10},{13,12},{... | collective-permute-start | bytes 13832 | tf_op jit(solution)/shard_map/ppermute | solution.py:15
  177.9 3.3 %collective-permute-start.4 = (bf16[1,16,128]{2,1,0:T(8,128)(2,1)S(1)}, bf16[1,16,128]{2,1,0:T(8,128)(2,1)S(1)}, u32[]{:S(2)}, u32[]{:S(2)}) collective-permute-start(bf16[1,16,128]{2,1,0:T(8,128)(2,1)S(1)} %get-tuple-element.80), channel_id=1, source_target_pairs={{0,4},{4,8},{8,12},{12,16},{16,20},{20,24},{24,28},{1,5},{5,9},{9,... | collective-permute-start | bytes 12296 | tf_op jit(solution)/shard_map/ppermute | solution.py:12
  179.2 4.9 %collective-permute-start.5 = (bf16[1,16,128]{2,1,0:T(8,128)(2,1)S(1)}, bf16[1,16,128]{2,1,0:T(8,128)(2,1)S(1)}, u32[]{:S(2)}, u32[]{:S(2)}) collective-permute-start(bf16[1,16,128]{2,1,0:T(8,128)(2,1)S(1)} %get-tuple-element.81), channel_id=1, source_target_pairs={{4,0},{8,4},{12,8},{16,12},{20,16},{24,20},{28,24},{5,1},{9,5},{13... | collective-permute-start | bytes 12296 | tf_op jit(solution)/shard_map/ppermute | solution.py:15
  184.1 9.0 %collective-permute-start.6 = (bf16[18,1,128]{2,1,0:T(2,128)(2,1)S(1)}, bf16[18,1,128]{2,1,0:T(2,128)(2,1)S(1)}, u32[]{:S(2)}, u32[]{:S(2)}) collective-permute-start(bf16[18,1,128]{2,1,0:T(2,128)(2,1)S(1)} %get-tuple-element.70), channel_id=1, source_target_pairs={{0,1},{1,2},{2,3},{4,5},{5,6},{6,7},{8,9},{9,10},{10,11},{12,13},{... | collective-permute-start | bytes 13832 | tf_op jit(solution)/shard_map/ppermute | solution.py:12
  186.2 7.0 %collective-permute-start.7 = (bf16[18,1,128]{2,1,0:T(2,128)(2,1)S(1)}, bf16[18,1,128]{2,1,0:T(2,128)(2,1)S(1)}, u32[]{:S(2)}, u32[]{:S(2)}) collective-permute-start(bf16[18,1,128]{2,1,0:T(2,128)(2,1)S(1)} %get-tuple-element.71), channel_id=1, source_target_pairs={{1,0},{2,1},{3,2},{5,4},{6,5},{7,6},{9,8},{10,9},{11,10},{13,12},{... | collective-permute-start | bytes 13832 | tf_op jit(solution)/shard_map/ppermute | solution.py:15
  285.6 7.9 %copy-start.4 = (f32[3,2]{0,1:T(2,128)}, f32[3,2]{0,1:T(2,128)S(1)}, u32[]{:S(2)}) copy-start(f32[3,2]{0,1:T(2,128)S(1)} %scatter.24) | copy-start | bytes 76
where the time goes:
time: 295 us; the launch traced here: 293 us
  blocking collectives  228 us (77%)
  matrix products  17.3 us (6%)
  starting transfers between devices  12.2 us (4%)
  other arithmetic  11 us (4%)
  between operations  9.67 us (3%)
  local copies, waits for them, and re-layouts  7.55 us (3%)
  waiting for transfers between devices  7.18 us (2%)
    psum x2, blocking collectives, body(): coeffs = lax.psum(partial_dots, ('gx', 'gy'))  85.4 us
    psum x2, blocking collectives, body(): length = jnp.sqrt(lax.psum(jnp.sum(image * image), ('gx', 'gy')))  80.4 us
    psum x1, blocking collectives, body(): start_len = jnp.sqrt(lax.psum(jnp.sum(rhs_field * rhs_field), ('gx', 'gy')))  42.2 us
    all_gather x2, blocking collectives, coarse_correct(): column = lax.all_gather(coarse, 'gy', axis=1, tiled=True)  20.6 us
    dot_general x2, matrix products, apply_operator(): jnp.einsum('ija,ijab->ijb', rounded, diag_blocks, preferred_element_type=...  11.4 us
    ppermute x4, waiting for transfers between devices, padded_2(): lax.ppermute(lax.slice_in_dim(block, 0, width, axis=dim), axis, backward)  7.11 us
    ppermute x4, starting transfers between devices, padded_2(): lax.ppermute(lax.slice_in_dim(block, block.shape[dim] - width, None, axis...  7.05 us
  transfers between devices with their start and end apart: 8, of which 2 were waited for; matrix products, arithmetic and copies ran while one was open for 4% of the time, Pallas kernels for 0%

commit v1 on v0

--- a/solution.py
+++ b/solution.py
@@ -79,7 +79,7 @@
         precon.append(precond)
         image = apply_operator(precond, diag_blocks, face_lift, face_state)
         partial_dots = jnp.stack([jnp.sum(vector * image) for vector in basis])
-        coeffs = lax.psum(partial_dots, ("gx", "gy"))
+        coeffs = lax.psum(lax.psum(partial_dots, "gy"), "gx")
         for index in range(step + 1):
             image = image - coeffs[index] * basis[index]
         length = jnp.sqrt(lax.psum(jnp.sum(image * image), ("gx", "gy")))

time: 295 us -> 258 us (0.87)
  blocking collectives: 228 us -> 188 us
    psum x2 -> x4, blocking collectives: 85.4 us -> 49.7 us  [body(): coeffs = lax.psum(lax.psum(partial_dots, 'gy'), 'gx')]
    psum x2, blocking collectives: 80.4 us -> 75.7 us  [body(): length = jnp.sqrt(lax.psum(jnp.sum(image * image), ('gx', 'gy')))]
  transfers between devices with their start and end apart: 8 -> 8, of which waited for: 2 -> 2; matrix products, arithmetic and copies ran while one was open for 4% -> 5% of each run, Pallas kernels for 0% -> 0%
where the time goes in v1:
time: 258 us; the launch traced here: 256 us
  blocking collectives  188 us (73%)
  matrix products  17.4 us (7%)
  starting transfers between devices  13.6 us (5%)
  other arithmetic  11.1 us (4%)
  between operations  9.67 us (4%)
  waiting for transfers between devices  8.36 us (3%)
  local copies, waits for them, and re-layouts  7.47 us (3%)
    psum x2, blocking collectives, body(): length = jnp.sqrt(lax.psum(jnp.sum(image * image), ('gx', 'gy')))  75.7 us
    psum x4, blocking collectives, body(): coeffs = lax.psum(lax.psum(partial_dots, 'gy'), 'gx')  49.7 us
    psum x1, blocking collectives, body(): start_len = jnp.sqrt(lax.psum(jnp.sum(rhs_field * rhs_field), ('gx', 'gy')))  42.2 us
    all_gather x2, blocking collectives, coarse_correct(): column = lax.all_gather(coarse, 'gy', axis=1, tiled=True)  20.6 us
    dot_general x2, matrix products, apply_operator(): jnp.einsum('ija,ijab->ijb', rounded, diag_blocks, preferred_element_type=...  11.4 us
    ppermute x4, starting transfers between devices, padded_2(): lax.ppermute(lax.slice_in_dim(block, block.shape[dim] - width, None, axis...  8.41 us
    ppermute x4, waiting for transfers between devices, padded_2(): lax.ppermute(lax.slice_in_dim(block, 0, width, axis=dim), axis, backward)  8.3 us
    ppermute x4, starting transfers between devices, padded_2(): lax.ppermute(lax.slice_in_dim(block, 0, width, axis=dim), axis, backward)  5.17 us
  transfers between devices with their start and end apart: 8, of which 2 were waited for; matrix products, arithmetic and copies ran while one was open for 5% of the time, Pallas kernels for 0%

profile of v1, /device:TPU:0, one launch (start us, length us, event | category | flops | bytes accessed | tf_op | source)
XLA Modules:
  0.0 255.6 jit_solution(16129806525222211507)
XLA Ops:
  0.6 1.6 multiply_reduce_fusion.7
  2.2 42.2 %psum.49 = f32[]{:T(128)} all-reduce(f32[]{:T(128)} %multiply_reduce_fusion.7), channel_id=1, replica_groups=mesh['gx'=8,'gy'=4] {'gx','gy'}, use_global_device_ids=true, to_apply=%region_1.0 | all-reduce | flops 1 | bytes 8 | tf_op jit(solution)/shard_map/psum | solution.py:73
  45.1 0.9 broadcast_divide_fusion.1
  46.0 1.7 fusion.20
  47.7 10.3 %all_gather.6 = f32[16,64,8]{0,2,1:T(8,128)S(1)} all-gather(f32[16,16,8]{0,2,1:T(8,128)S(1)} %fusion.20), channel_id=1, replica_groups=mesh['gx'=8,'gy'=4] {'gy'}, dimensions={1}, use_global_device_ids=true | all-gather | bytes 40960 | tf_op jit(solution)/shard_map/all_gather | solution.py:49
  58.3 1.1 multiply_reduce_fusion.1
  59.4 1.1 fusion.36
  60.5 1.3 collective-permute-start
  61.8 1.3 collective-permute-start.1
  63.1 0.9 fusion.32
  64.1 5.7 %fusion.18 = f32[16,16,1,128]{3,2,1,0:T(1,128)S(1)} fusion(bf16[16,16,128,128]{3,2,1,0:T(8,128)(2,1)} %param.17, bf16[16,16,128,1]{2,1,0,3:T(8,128)(2,1)S(1)} %bitcast.67), kind=kOutput, calls=%fused_computation.28 | convolution fusion | flops 8388608 | bytes 8585216 | tf_op jit(solution)/shard_map/ija,ijab->ijb/dot_general | solution.py:22
  69.9 2.5 collective-permute-start.2
  72.4 1.3 collective-permute-start.3
  73.7 4.2 %collective-permute-done.3 = bf16[18,1,128]{2,1,0:T(2,128)(2,1)S(1)} collective-permute-done((bf16[18,1,128]{2,1,0:T(2,128)(2,1)S(1)}, bf16[18,1,128]{2,1,0:T(2,128)(2,1)S(1)}, u32[]{:S(2)}, u32[]{:S(2)}) %collective-permute-start.3) | collective-permute-done | bytes 4640 | tf_op jit(solution)/shard_map/ppermute | solution.py:15
  79.7 10.4 %psum.50 = f32[1]{0:T(128)} all-reduce(f32[1]{0:T(128)} %bitcast.14), channel_id=1, replica_groups=mesh['gx'=8,'gy'=4] {'gy'}, use_global_device_ids=true, to_apply=%region_4.5 | all-reduce | flops 1 | bytes 8 | tf_op jit(solution)/shard_map/psum | solution.py:82
  90.1 15.5 %psum.51 = f32[1]{0:T(128)} all-reduce(f32[1]{0:T(128)} %psum.50), channel_id=1, replica_groups=mesh['gx'=8,'gy'=4] {'gx'}, use_global_device_ids=true, to_apply=%region_5.6 | all-reduce | flops 1 | bytes 8 | tf_op jit(solution)/shard_map/psum | solution.py:82
  105.6 1.3 multiply_reduce_fusion.5
  106.9 37.8 %psum.52 = f32[]{:T(128)} all-reduce(f32[]{:T(128)} %multiply_reduce_fusion.5), channel_id=1, replica_groups=mesh['gx'=8,'gy'=4] {'gx','gy'}, use_global_device_ids=true, to_apply=%region_7.8 | all-reduce | flops 1 | bytes 8 | tf_op jit(solution)/shard_map/psum | solution.py:85
  146.1 1.0 fusion.16
  147.1 10.3 %all_gather.7 = f32[16,64,8]{0,2,1:T(8,128)S(1)} all-gather(f32[16,16,8]{0,2,1:T(8,128)S(1)} %fusion.16), channel_id=1, replica_groups=mesh['gx'=8,'gy'=4] {'gy'}, dimensions={1}, use_global_device_ids=true | all-gather | bytes 40960 | tf_op jit(solution)/shard_map/all_gather | solution.py:49
  158.2 1.3 collective-permute-start.4
  159.5 1.3 collective-permute-start.5
  160.8 4.1 %collective-permute-done.5 = bf16[1,16,128]{2,1,0:T(8,128)(2,1)S(1)} collective-permute-done((bf16[1,16,128]{2,1,0:T(8,128)(2,1)S(1)}, bf16[1,16,128]{2,1,0:T(8,128)(2,1)S(1)}, u32[]{:S(2)}, u32[]{:S(2)}) %collective-permute-start.5) | collective-permute-done | bytes 4128 | tf_op jit(solution)/shard_map/ppermute | solution.py:15
  164.9 3.4 %collective-permute-start.6 = (bf16[18,1,128]{2,1,0:T(2,128)(2,1)S(1)}, bf16[18,1,128]{2,1,0:T(2,128)(2,1)S(1)}, u32[]{:S(2)}, u32[]{:S(2)}) collective-permute-start(bf16[18,1,128]{2,1,0:T(2,128)(2,1)S(1)} %get-tuple-element.70), channel_id=1, source_target_pairs={{0,1},{1,2},{2,3},{4,5},{5,6},{6,7},{8,9},{9,10},{10,11},{12,13},{... | collective-permute-start | bytes 13832 | tf_op jit(solution)/shard_map/ppermute | solution.py:12
  168.3 1.3 collective-permute-start.7
  169.6 5.7 %fusion.14 = f32[16,16,1,128]{3,2,1,0:T(1,128)S(1)} fusion(bf16[16,16,128,128]{3,2,1,0:T(8,128)(2,1)} %param.17, bf16[16,16,128,1]{2,1,0,3:T(8,128)(2,1)S(1)} %bitcast.68), kind=kOutput, calls=%fused_computation.24 | convolution fusion | flops 8388608 | bytes 8585216 | tf_op jit(solution)/shard_map/ija,ijab->ijb/dot_general | solution.py:22
  177.2 1.3 pad_maximum_fusion.22
  179.1 10.1 %psum.53 = f32[2]{0:T(128)S(1)} all-reduce(f32[2]{0:T(128)S(1)} %pad_maximum_fusion.22), channel_id=1, replica_groups=mesh['gx'=8,'gy'=4] {'gy'}, use_global_device_ids=true, to_apply=%region_11.12 | all-reduce | flops 2 | bytes 16 | tf_op jit(solution)/shard_map/psum | solution.py:82
  189.9 13.7 %psum.54 = f32[2]{0:T(128)S(1)} all-reduce(f32[2]{0:T(128)S(1)} %psum.53), channel_id=1, replica_groups=mesh['gx'=8,'gy'=4] {'gx'}, use_global_device_ids=true, to_apply=%region_12.13 | all-reduce | flops 2 | bytes 16 | tf_op jit(solution)/shard_map/psum | solution.py:82
  204.1 2.0 multiply_reduce_fusion.2
  206.3 38.0 %psum.55 = f32[]{:T(128)} all-reduce(f32[]{:T(128)} %multiply_reduce_fusion.2), channel_id=1, replica_groups=mesh['gx'=8,'gy'=4] {'gx','gy'}, use_global_device_ids=true, to_apply=%region_14.15 | all-reduce | flops 1 | bytes 8 | tf_op jit(solution)/shard_map/psum | solution.py:85
  244.9 1.9 scatter.20
  (66 shorter events, 9.6 us)
Async XLA Ops:
  0.6 78.2 %copy-start = (bf16[4,128,128]{2,1,0:T(8,128)(2,1)S(1)}, bf16[4,128,128]{2,1,0:T(8,128)(2,1)}, u32[]{:S(2)}) copy-start(bf16[4,128,128]{2,1,0:T(8,128)(2,1)} %param.18) | copy-start | bytes 393220
  60.5 9.3 %collective-permute-start = (bf16[1,16,128]{2,1,0:T(8,128)(2,1)S(1)}, bf16[1,16,128]{2,1,0:T(8,128)(2,1)S(1)}, u32[]{:S(2)}, u32[]{:S(2)}) collective-permute-start(bf16[1,16,128]{2,1,0:T(8,128)(2,1)S(1)} %get-tuple-element.82), channel_id=1, source_target_pairs={{0,4},{4,8},{8,12},{12,16},{16,20},{20,24},{24,28},{1,5},{5,9},{9,... | collective-permute-start | bytes 12296 | tf_op jit(solution)/shard_map/ppermute | solution.py:12
  61.8 8.1 %collective-permute-start.1 = (bf16[1,16,128]{2,1,0:T(8,128)(2,1)S(1)}, bf16[1,16,128]{2,1,0:T(8,128)(2,1)S(1)}, u32[]{:S(2)}, u32[]{:S(2)}) collective-permute-start(bf16[1,16,128]{2,1,0:T(8,128)(2,1)S(1)} %get-tuple-element.83), channel_id=1, source_target_pairs={{4,0},{8,4},{12,8},{16,12},{20,16},{24,20},{28,24},{5,1},{9,5},{13... | collective-permute-start | bytes 12296 | tf_op jit(solution)/shard_map/ppermute | solution.py:15
  64.1 41.5 %copy-start.1 = (f32[16,16,128]{2,1,0:T(8,128)S(1)}, f32[16,16,128]{2,1,0:T(8,128)}, u32[]{:S(2)}) copy-start(f32[16,16,128]{2,1,0:T(8,128)} %param.16) | copy-start | bytes 393220
  64.1 81.9 %copy-start.3 = (f32[128,8]{0,1:T(8,128)S(1)}, f32[128,8]{0,1:T(8,128)}, u32[]{:S(2)}) copy-start(f32[128,8]{0,1:T(8,128)} %param.20) | copy-start | bytes 12292
  64.1 93.5 %copy-start.2 = (f32[16,16,8,8]{1,3,2,0:T(8,128)S(1)}, f32[16,16,8,8]{1,3,2,0:T(8,128)}, u32[]{:S(2)}) copy-start(f32[16,16,8,8]{1,3,2,0:T(8,128)} %param.21) | copy-start | bytes 196612
  69.9 3.8 %collective-permute-start.2 = (bf16[18,1,128]{2,1,0:T(2,128)(2,1)S(1)}, bf16[18,1,128]{2,1,0:T(2,128)(2,1)S(1)}, u32[]{:S(2)}, u32[]{:S(2)}) collective-permute-start(bf16[18,1,128]{2,1,0:T(2,128)(2,1)S(1)} %get-tuple-element.74), channel_id=1, source_target_pairs={{0,1},{1,2},{2,3},{4,5},{5,6},{6,7},{8,9},{9,10},{10,11},{12,13},{... | collective-permute-start | bytes 13832 | tf_op jit(solution)/shard_map/ppermute | solution.py:12
  72.4 5.6 %collective-permute-start.3 = (bf16[18,1,128]{2,1,0:T(2,128)(2,1)S(1)}, bf16[18,1,128]{2,1,0:T(2,128)(2,1)S(1)}, u32[]{:S(2)}, u32[]{:S(2)}) collective-permute-start(bf16[18,1,128]{2,1,0:T(2,128)(2,1)S(1)} %get-tuple-element.75), channel_id=1, source_target_pairs={{1,0},{2,1},{3,2},{5,4},{6,5},{7,6},{9,8},{10,9},{11,10},{13,12},{... | collective-permute-start | bytes 13832 | tf_op jit(solution)/shard_map/ppermute | solution.py:15
  158.2 2.6 %collective-permute-start.4 = (bf16[1,16,128]{2,1,0:T(8,128)(2,1)S(1)}, bf16[1,16,128]{2,1,0:T(8,128)(2,1)S(1)}, u32[]{:S(2)}, u32[]{:S(2)}) collective-permute-start(bf16[1,16,128]{2,1,0:T(8,128)(2,1)S(1)} %get-tuple-element.80), channel_id=1, source_target_pairs={{0,4},{4,8},{8,12},{12,16},{16,20},{20,24},{24,28},{1,5},{5,9},{9,... | collective-permute-start | bytes 12296 | tf_op jit(solution)/shard_map/ppermute | solution.py:12
  159.5 5.4 %collective-permute-start.5 = (bf16[1,16,128]{2,1,0:T(8,128)(2,1)S(1)}, bf16[1,16,128]{2,1,0:T(8,128)(2,1)S(1)}, u32[]{:S(2)}, u32[]{:S(2)}) collective-permute-start(bf16[1,16,128]{2,1,0:T(8,128)(2,1)S(1)} %get-tuple-element.81), channel_id=1, source_target_pairs={{4,0},{8,4},{12,8},{16,12},{20,16},{24,20},{28,24},{5,1},{9,5},{13... | collective-permute-start | bytes 12296 | tf_op jit(solution)/shard_map/ppermute | solution.py:15
  164.9 10.3 %collective-permute-start.6 = (bf16[18,1,128]{2,1,0:T(2,128)(2,1)S(1)}, bf16[18,1,128]{2,1,0:T(2,128)(2,1)S(1)}, u32[]{:S(2)}, u32[]{:S(2)}) collective-permute-start(bf16[18,1,128]{2,1,0:T(2,128)(2,1)S(1)} %get-tuple-element.70), channel_id=1, source_target_pairs={{0,1},{1,2},{2,3},{4,5},{5,6},{6,7},{8,9},{9,10},{10,11},{12,13},{... | collective-permute-start | bytes 13832 | tf_op jit(solution)/shard_map/ppermute | solution.py:12
  168.3 7.0 %collective-permute-start.7 = (bf16[18,1,128]{2,1,0:T(2,128)(2,1)S(1)}, bf16[18,1,128]{2,1,0:T(2,128)(2,1)S(1)}, u32[]{:S(2)}, u32[]{:S(2)}) collective-permute-start(bf16[18,1,128]{2,1,0:T(2,128)(2,1)S(1)} %get-tuple-element.71), channel_id=1, source_target_pairs={{1,0},{2,1},{3,2},{5,4},{6,5},{7,6},{9,8},{10,9},{11,10},{13,12},{... | collective-permute-start | bytes 13832 | tf_op jit(solution)/shard_map/ppermute | solution.py:15
  247.8 7.9 %copy-start.4 = (f32[3,2]{0,1:T(2,128)}, f32[3,2]{0,1:T(2,128)S(1)}, u32[]{:S(2)}) copy-start(f32[3,2]{0,1:T(2,128)S(1)} %scatter.24) | copy-start | bytes 76
